TPU v7x, 32 devices: a whole 2x2x4 slice. The times are simulated.
32 devices in a mesh: gen: 4 (over y, core), rows: 4 (over z), img: 2 (over x).
Axes of the slice: x: 2, y: 2, z: 4, core: 2. Of those that a mesh axis runs over, the one named last changes fastest.
Arguments:
- center: bfloat16 [2, 32, 32, 128], P('img', 'rows'), may hold values from -6 to 6
- gens: bfloat16 [2, 256, 32, 32, 128], P('img', 'gen', 'rows'), may hold values from -6 to 6
- weight: bfloat16 [3, 3, 128, 128], replicated, may hold values from -0.1875 to 0.1875
- bias: float32 [128], replicated, may hold values from -3 to 3
- radius: float32 [2, 32, 32, 128], P('img', 'rows'), may hold values from 1 to 4
- state: int32 [2, 32, 32, 128], P('img', 'rows'), may hold values from 0 to 2, as said below
- unstable: int32 [2, 16384], P('img'), may hold values from 0 to 131071, as said below
- d_center: float32 [2, 32, 32, 128], P('img', 'rows'), may hold values from -6 to 6
- d_gens: bfloat16 [2, 256, 32, 32, 128], P('img', 'gen', 'rows'), may hold values from -6 to 6
- d_new: float32 [2, 16384], P('img'), may hold values from -6 to 6
Outputs:
- grad_center: bfloat16 [2, 32, 32, 128], P('img', 'rows')
- grad_gens: bfloat16 [2, 256, 32, 32, 128], P('img', 'gen', 'rows')
- grad_weight: float32 [3, 3, 128, 128], replicated
- grad_bias: float32 [128], replicated
- grad_radius: float32 [2, 16384], P('img', 'rows')
Inputs may be any that keep to these rules, and one draw needn't show every extreme that they name: `unstable`: each row lists 16384 different neurons of its image; 0 and the last neuron are always listed. `state`: 2 exactly at the neurons that the image's row of unstable lists, else 0 or 1.
All inputs are finite; a program needn't handle non-finite values.
Results may differ from a plain program's by a relative error of at most 0.0049.
Values may be sent and summed in bfloat16 or wider, within the bound.
A program may use at most 128 MiB of HBM per device.

v0:
```python
import jax
import jax.numpy as jnp
from jax import lax
from jax.sharding import PartitionSpec as P

DIMS = ("NHWC", "HWIO", "NHWC")
EXACT = lax.Precision.HIGHEST


def with_halo(array, sides, width):
    for axis, dim in sides:
        devices, length = (lax.axis_size(axis), array.shape[dim])
        up = [(i, (i + 1) % devices) for i in range(devices - 1)]
        down = [(j, i) for i, j in up]
        last = lax.slice_in_dim(array, length - width, length, axis=dim)
        leading = lax.slice_in_dim(array, 0, width, axis=dim)
        before = lax.ppermute(last, axis, up)
        after = lax.ppermute(leading, axis, down)
        array = jnp.concatenate([before, array, after], axis=dim)
    return array


def conv_band(field, kernel):
    return lax.conv_general_dilated(
        field,
        kernel,
        (1, 1),
        ((0, 0), (1, 1)),
        dimension_numbers=DIMS,
        preferred_element_type=jnp.float32,
    )


def lookup_tables(ids, first_cell, places, chans):
    local = ids - first_cell
    place_of = local // chans
    chan_of = ids % chans
    place_table = (place_of[:, None] == jnp.arange(places, dtype=jnp.int32)[None, :]).astype(
        jnp.float32
    )
    chan_table = (chan_of[:, None] == jnp.arange(chans, dtype=jnp.int32)[None, :]).astype(
        jnp.float32
    )
    return (place_table, chan_table)


def listed_terms(ids, values, first_row, row_count, width, chans):
    places = row_count * width
    place_table, chan_table = lookup_tables(ids, first_row * width * chans, places, chans)
    weighted = place_table * values[:, None]
    spread = lax.dot_general(
        weighted,
        chan_table,
        (((0,), (0,)), ((), ())),
        precision=EXACT,
        preferred_element_type=jnp.float32,
    )
    return spread.reshape(row_count, width, chans)


def picked_values(ids, field, first_cell, chans):
    place_table, chan_table = lookup_tables(ids, first_cell, field.shape[0], chans)
    rows_of = jnp.dot(place_table, field, precision=EXACT, preferred_element_type=jnp.float32)
    return jnp.sum(rows_of * chan_table, axis=1)


def relu_terms(y_center, products, radius, state, d_center, extra):
    unstable_mask = state == 2
    safe_r = jnp.where(unstable_mask, radius, 1.0)
    two_r = 2.0 * safe_r
    slope = jnp.where(unstable_mask, (y_center + safe_r) / two_r, jnp.where(state == 1, 1.0, 0.0))
    d_mu = d_center + extra
    d_lam = d_center * y_center + products
    d_yc = slope * d_center + jnp.where(unstable_mask, (d_lam - d_mu * y_center) / two_r, 0.0)
    d_rad = jnp.where(
        unstable_mask,
        -d_lam * y_center / (two_r * safe_r)
        + d_mu * (0.25 + y_center * y_center / (two_r * two_r)),
        0.0,
    )
    return (slope, d_yc, d_rad)


def on_device(center, gens, weight, bias, radius, state, unstable, d_center, d_gens, d_new):
    band = center.shape[1]
    width = center.shape[2]
    chans = center.shape[3]
    count = gens.shape[1]
    row_pos = lax.axis_index("rows")
    flipped = jnp.transpose(weight[::-1, ::-1], (0, 1, 3, 2))
    ids = unstable[0]
    values = d_new[0]
    stacked = jnp.concatenate([center, gens[0]], axis=0)
    padded = with_halo(stacked, (("rows", 1),), 1)
    forward = conv_band(padded, weight)
    y_center = forward[0] + bias
    partial_sum = jnp.sum(d_gens[0].astype(jnp.float32) * forward[1:], axis=0)
    products = lax.psum(partial_sum, "gen")
    extra = listed_terms(ids, values, row_pos * band, band, width, chans)
    slope, d_yc, d_rad = relu_terms(y_center, products, radius[0], state[0], d_center[0], extra)
    d_first = jnp.concatenate(
        [
            d_yc.astype(jnp.bfloat16)[None],
            (slope * d_gens[0].astype(jnp.float32)).astype(jnp.bfloat16),
        ],
        axis=0,
    )
    d_padded = with_halo(d_first, (("rows", 1),), 1)
    backward = conv_band(d_padded, flipped).astype(jnp.bfloat16)
    grad_center = backward[0][None]
    grad_gens = backward[1:][None]
    d_rows = d_padded[:, 1:-1].reshape(count + 1, -1, chans)
    wide_inputs = jnp.pad(padded, ((0, 0), (0, 0), (1, 1), (0, 0)))
    leader = (lax.axis_index("gen") == 0).astype(jnp.float32)
    contract = (((0,), (0,)), ((), ()))
    taps = []
    for row_off in range(3):
        for col_off in range(3):
            window = wide_inputs[:, row_off : row_off + band, col_off : col_off + width, :].reshape(
                count + 1, -1, chans
            )
            gen_part = lax.dot_general(
                window[1:].reshape(-1, chans),
                d_rows[1:].reshape(-1, chans),
                contract,
                preferred_element_type=jnp.float32,
            )
            center_part = lax.dot_general(
                window[0], d_rows[0], contract, preferred_element_type=jnp.float32
            )
            taps.append(gen_part + leader * center_part)
    grad_w_local = jnp.stack(taps).reshape(3, 3, chans, chans)
    grad_b_local = leader * jnp.sum(d_yc, axis=(0, 1))
    totals = lax.psum((grad_w_local, grad_b_local), ("gen", "rows", "img"))
    positions = float(band * lax.axis_size("rows") * width * lax.axis_size("img"))
    grad_weight = totals[0] / positions
    grad_bias = totals[1] / positions
    block = unstable.shape[1] // lax.axis_size("rows")
    whole = lax.all_gather(d_rad[None], "rows", axis=1, tiled=True)
    mine = lax.dynamic_slice_in_dim(ids, row_pos * block, block, 0)
    grad_radius = picked_values(mine, whole.reshape(-1, chans), 0, chans)[None]
    return (grad_center, grad_gens, grad_weight, grad_bias, grad_radius)


def solution(mesh):
    return jax.shard_map(
        on_device,
        mesh=mesh,
        in_specs=(
            P("img", "rows", None, None),
            P("img", "gen", "rows", None, None),
            P(),
            P(),
            P("img", "rows", None, None),
            P("img", "rows", None, None),
            P("img", None),
            P("img", "rows", None, None),
            P("img", "gen", "rows", None, None),
            P("img", None),
        ),
        out_specs=(
            P("img", "rows", None, None),
            P("img", "gen", "rows", None, None),
            P(),
            P(),
            P("img", "rows"),
        ),
        check_vma=False,
    )
```

profile of v0, /device:TPU:0, one launch (start us, length us, event | category | flops | bytes accessed | tf_op | source)
XLA Modules:
  0.0 312.3 jit_solution(15731429385624743366)
XLA Ops:
  7.2 4.9 %copy.104 = bf16[1,64,8,32,128]{4,1,3,2,0:T(8,128)(2,1)S(1)} copy(bf16[1,64,8,32,128]{4,3,2,1,0:T(8,128)(2,1)} %param.11) | data formatting | bytes 8388608 | tf_op args[1]
  12.3 1.9 copy-done.1
  14.8 5.0 %collective-permute-start = (bf16[65,1,32,128]{3,2,1,0:T(8,128)(2,1)S(1)}, bf16[65,1,32,128]{3,2,1,0:T(8,128)(2,1)S(1)}, u32[]{:S(2)}, u32[]{:S(2)}) collective-permute-start(bf16[65,1,32,128]{3,2,1,0:T(8,128)(2,1)S(1)} %copy.60), channel_id=1, source_target_pairs={{0,2},{2,4},{4,6},{1,3},{3,5},{5,7},{8,10},{10,12},{12,14},{9,11},... | collective-permute-start | bytes 1597448 | tf_op jit(solution)/shard_map/ppermute | solution.py:17
  21.3 4.7 %iota_compare_fusion.14 = pred[16384,128]{1,0:T(32,128)(4,1)} fusion(s32[16384]{0:T(1024)S(1)} %get-tuple-element.44), kind=kLoop, calls=%fused_computation.13.clone.clone.2 | loop fusion | flops 2097152 | bytes 2162688 | tf_op jit(solution)/shard_map/dot_general | solution.py:51
  26.0 19.7 %fusion = f32[256,128]{1,0:T(8,128)S(1)} fusion(f32[16384]{0:T(1024)S(1)} %bitcast.266, s32[16384]{0:T(1024)S(1)} %get-tuple-element.45, pred[16384,128]{1,0:T(32,128)(4,1)} %iota_compare_fusion.14), kind=kOutput, calls=%fused_computation.1 | convolution fusion | flops 6450839552 | bytes 2359296 | tf_op jit(solution)/shard_map/dot_general | solution.py:51
  46.2 4.9 %pad_maximum_fusion = bf16[65,10,32,128]{3,0,2,1:T(8,128)(2,1)} fusion(bf16[65,1,32,128]{3,0,2,1:T(8,128)(2,1)S(1)} %copy.63, bf16[64,8,32,128]{3,0,2,1:T(8,128)(2,1)S(1)} %bitcast.232, bf16[1,8,32,128]{3,0,2,1:T(2,128)(2,1)S(1)} %copy.59, bf16[65,1,32,128]{3,0,2,1:T(8,128)(2,1)S(1)} %copy.62), kind=kLoop, calls=%fused_computation.17 | loop fusion | flops 21299200 | bytes 10649600 | tf_op jit(solution)/shard_map/concatenate | solution.py:19
  51.1 8.2 %pad_maximum_fusion.1 = (bf16[65,9,32,128]{3,0,2,1:T(8,128)(2,1)}, bf16[65,9,32,128]{3,0,2,1:T(8,128)(2,1)}) fusion(bf16[65,1,32,128]{3,0,2,1:T(8,128)(2,1)S(1)} %copy.63, bf16[64,8,32,128]{3,0,2,1:T(8,128)(2,1)S(1)} %bitcast.233, bf16[1,8,32,128]{3,0,2,1:T(2,128)(2,1)S(1)} %copy.59, bf16[65,1,32,128]{3,0,2,1:T(8,128)(2,1)S(1)} %copy.62), kind=kLoop, calls=%fused_computation.27 | loop fusion | flops 28753920 | bytes 14909440 | tf_op jit(solution)/shard_map/concatenate | solution.py:19
  59.3 12.7 %fusion.179 = f32[65,8,32,128]{3,0,2,1:T(8,128)S(1)} fusion(bf16[3,3,128,128]{3,2,1,0:T(8,128)(2,1)S(1)} %copy-done, bf16[65,1,32,128]{3,0,2,1:T(8,128)(2,1)S(1)} %copy.63, bf16[64,8,32,128]{3,0,2,1:T(8,128)(2,1)S(1)} %bitcast.234, bf16[1,8,32,128]{3,0,2,1:T(2,128)(2,1)S(1)} %copy.59, bf16[65,1,32,128]{3,0,2,1:T(8,128)(2,1)S(1)} %copy.62), kind=kOutput, calls=%fused_computation.172 | convolution fusion | flops 4826398720 | bytes 14139392 | tf_op jit(solution)/shard_map/conv_general_dilated | solution.py:24
  72.1 3.9 %fusion.5 = f32[8,32,128]{2,1,0:T(8,128)} fusion(f32[65,8,32,128]{3,0,2,1:T(8,128)S(1)} %fusion.179, bf16[1,64,8,32,128]{4,3,2,1,0:T(8,128)(2,1)S(1)} %copy-done.4), kind=kLoop, calls=%fused_computation.9 | loop fusion | flops 6258688 | bytes 12713984 | tf_op jit(solution)/shard_map/reduce_sum | solution.py:97
  76.1 3.3 %pad_slice_fusion = (bf16[1,8,32,128]{3,0,2,1:T(2,128)(2,1)S(1)}, bf16[1,8,32,128]{3,0,2,1:T(2,128)(2,1)S(1)}, bf16[1,8,32,128]{3,0,2,1:T(2,128)(2,1)S(1)}, bf16...) fusion(bf16[65,10,32,128]{3,0,2,1:T(8,128)(2,1)} %pad_maximum_fusion), kind=kLoop, calls=%fused_computation.110 | loop fusion | bytes 5718016 | tf_op jit(solution)/shard_map/slice | solution.py:129
  79.9 30.4 %all-reduce.4.cloned.1.call-done = f32[8,32,128]{2,1,0:T(8,128)} async-done(((f32[8,32,128]{2,1,0:T(8,128)}), f32[8,32,128]{2,1,0:T(8,128)}) %all-reduce.4.cloned.1.call-update) | async-done | bytes 131088 | tf_op jit(solution)/shard_map/psum | solution.py:98
  113.2 7.4 %fusion.6 = bf16[64,8,32,128]{3,0,2,1:T(8,128)(2,1)} fusion(f32[8,32,128]{2,1,0:T(8,128)S(1)} %fusion.157, bf16[1,64,8,32,128]{4,3,2,1,0:T(8,128)(2,1)} %param.18), kind=kLoop, calls=%fused_computation.10 | loop fusion | flops 6291456 | bytes 8519680 | tf_op jit(solution)/shard_map/convert_element_type | solution.py:104
  120.6 9.4 %fusion.73 = f32[128,128]{1,0:T(8,128)S(1)} fusion(f32[8,32,128]{2,1,0:T(8,128)S(1)} %fusion.157, bf16[1,64,8,32,128]{4,3,2,1,0:T(8,128)(2,1)S(1)} %copy-done.5, bf16[1,64,8,32,128]{4,3,2,1,0:T(8,128)(2,1)S(1)} %copy-done.7), kind=kOutput, calls=%fused_computation.74 | convolution fusion | flops 543162368 | bytes 8585216 | tf_op jit(solution)/shard_map/dot_general | solution.py:122
  131.9 5.2 %fusion.145 = f32[9,128,128]{2,1,0:T(8,128)S(1)} fusion(f32[128,128]{1,0:T(8,128)S(1)} %convolution_multiply_fusion.8, bf16[64,8,32,128]{3,0,2,1:T(8,128)(2,1)} %fusion.6, bf16[65,10,32,128]{3,0,2,1:T(8,128)(2,1)} %pad_maximum_fusion), kind=kOutput, calls=%fused_computation.98 | convolution fusion | flops 536887296 | bytes 9650176 | tf_op jit(solution)/shard_map/dot_general | solution.py:122
  137.0 4.0 %fusion.91 = f32[9,128,128]{2,1,0:T(8,128)S(1)} fusion(f32[9,128,128]{2,1,0:T(8,128)S(1)} %fusion.145, f32[128,128]{1,0:T(8,128)S(1)} %convolution_multiply_fusion.7, bf16[64,8,32,128]{3,0,2,1:T(8,128)(2,1)S(1)} %copy-done.6, bf16[65,9,32,128]{3,0,2,1:T(8,128)(2,1)} %get-tuple-element.37), kind=kOutput, calls=%fused_computation.80 | convolution fusion | flops 536887296 | bytes 8519680 | tf_op jit(solution)/shard_map/dot_general | solution.py:122
  153.1 3.4 %collective-permute-start.2 = (bf16[65,1,32,128]{3,2,1,0:T(8,128)(2,1)S(1)}, bf16[65,1,32,128]{3,2,1,0:T(8,128)(2,1)S(1)}, u32[]{:S(2)}, u32[]{:S(2)}) collective-permute-start(bf16[65,1,32,128]{3,2,1,0:T(8,128)(2,1)S(1)} %copy.67), channel_id=1, source_target_pairs={{0,2},{2,4},{4,6},{1,3},{3,5},{5,7},{8,10},{10,12},{12,14},{9,11},... | collective-permute-start | bytes 1597448 | tf_op jit(solution)/shard_map/ppermute | solution.py:17
  157.9 29.8 %all-gather = f32[32,32,128]{2,1,0:T(8,128)S(1)} all-gather(f32[8,32,128]{2,1,0:T(8,128)S(1)} %get-tuple-element.25), channel_id=2, replica_groups=mesh['gen'=4,'rows'=4,'img'=2] {'rows'}, dimensions={0}, use_global_device_ids=true | all-gather | bytes 655360 | tf_op jit(solution)/shard_map/all_gather | solution.py:139
  187.7 10.2 %fusion.46 = f32[4096]{0:T(1024)} fusion(f32[1024,128]{1,0:T(8,128)S(1)} %bitcast.254, s32[4096]{0:T(1024)S(1)} %get-tuple-element.47, s32[4096]{0:T(1024)S(1)} %get-tuple-element.46), kind=kOutput, calls=%fused_computation.54 | convolution fusion | flops 6448214016 | bytes 573440 | tf_op jit(solution)/shard_map/dot_general | solution.py:63
  197.9 37.7 %psum.23 = f32[128]{0:T(128)S(1)} all-reduce(f32[128]{0:T(128)S(1)} %broadcast_multiply_fusion.2), channel_id=1, replica_groups=mesh['gen'=4,'rows'=4,'img'=2] {'gen','rows','img'}, use_global_device_ids=true, to_apply=%region_4.5 | all-reduce | flops 128 | bytes 1024 | tf_op jit(solution)/shard_map/psum | solution.py:134
  236.1 44.6 %all-reduce.6.cloned.1.call-done = f32[3,3,128,128]{3,2,1,0:T(8,128)} async-done(((f32[3,3,128,128]{3,2,1,0:T(8,128)}), f32[3,3,128,128]{3,2,1,0:T(8,128)}) %all-reduce.6.cloned.1.call-update) | async-done | bytes 589840 | tf_op jit(solution)/shard_map/psum | solution.py:134
  280.7 1.9 broadcast_multiply_fusion
  283.0 14.4 %fusion.43 = bf16[65,8,32,128]{3,0,2,1:T(8,128)(2,1)S(1)} fusion(bf16[3,3,128,128]{3,2,1,0:T(8,128)(2,1)S(1)} %copy-done, bf16[65,1,32,128]{3,0,2,1:T(8,128)(2,1)S(1)} %copy.70, bf16[64,8,32,128]{3,0,2,1:T(8,128)(2,1)} %fusion.6, bf16[1,8,32,128]{3,0,2,1:T(2,128)(2,1)S(1)} %copy.66, bf16[65,1,32,128]{3,0,2,1:T(8,128)(2,1)S(1)} %copy.69), kind=kOutput, calls=%fused_computation.52 | convolution fusion | flops 4828528640 | bytes 9879552 | tf_op jit(solution)/shard_map/conv_general_dilated | solution.py:24
  297.4 2.4 slice_bitcast_fusion
  299.9 4.7 %copy.75 = bf16[1,64,8,32,128]{4,3,2,1,0:T(8,128)(2,1)} copy(bf16[1,64,8,32,128]{4,1,3,2,0:T(8,128)(2,1)S(1)} %slice_bitcast_fusion) | data formatting | bytes 8388608
  (100 shorter events, 22.9 us)
Async XLA Ops:
  7.2 52.1 %copy-start = (bf16[3,3,128,128]{3,2,1,0:T(8,128)(2,1)S(1)}, bf16[3,3,128,128]{3,2,1,0:T(8,128)(2,1)}, u32[]{:S(2)}) copy-start(bf16[3,3,128,128]{3,2,1,0:T(8,128)(2,1)} %param.12) | copy-start | bytes 884740
  7.2 5.0 %copy-start.12 = (bf16[1,8,32,128]{3,2,1,0:T(8,128)(2,1)S(1)}, bf16[1,8,32,128]{3,2,1,0:T(8,128)(2,1)}, u32[]{:S(2)}) copy-start(bf16[1,8,32,128]{3,2,1,0:T(8,128)(2,1)} %param.10) | copy-start | bytes 196612
  7.2 103.1 %all-reduce.4.cloned.1.call-start = ((), (), s32[]{:S(2)}) async-start(), calls=%async_computation | async-start | bytes 262144 | tf_op jit(solution)/shard_map/psum | solution.py:98
  12.2 2.0 copy-start.1
  12.2 9.0 %copy-start.13 = (s32[1,16384]{1,0:T(1,128)S(1)}, s32[1,16384]{1,0:T(1,128)}, u32[]{:S(2)}) copy-start(s32[1,16384]{1,0:T(1,128)} %param.16) | copy-start | bytes 196612
  12.2 13.8 %copy-start.15 = (f32[1,16384]{1,0:T(1,128)S(1)}, f32[1,16384]{1,0:T(1,128)}, u32[]{:S(2)}) copy-start(f32[1,16384]{1,0:T(1,128)} %param.19) | copy-start | bytes 196612
  14.8 31.0 %collective-permute-start = (bf16[65,1,32,128]{3,2,1,0:T(8,128)(2,1)S(1)}, bf16[65,1,32,128]{3,2,1,0:T(8,128)(2,1)S(1)}, u32[]{:S(2)}, u32[]{:S(2)}) collective-permute-start(bf16[65,1,32,128]{3,2,1,0:T(8,128)(2,1)S(1)} %copy.60), channel_id=1, source_target_pairs={{0,2},{2,4},{4,6},{1,3},{3,5},{5,7},{8,10},{10,12},{12,14},{9,11},... | collective-permute-start | bytes 1597448 | tf_op jit(solution)/shard_map/ppermute | solution.py:17
  19.9 26.1 %collective-permute-start.1 = (bf16[65,1,32,128]{3,2,1,0:T(8,128)(2,1)S(1)}, bf16[65,1,32,128]{3,2,1,0:T(8,128)(2,1)S(1)}, u32[]{:S(2)}, u32[]{:S(2)}) collective-permute-start(bf16[65,1,32,128]{3,2,1,0:T(8,128)(2,1)S(1)} %copy.61), channel_id=1, source_target_pairs={{2,0},{4,2},{6,4},{3,1},{5,3},{7,5},{10,8},{12,10},{14,12},{11,9},... | collective-permute-start | bytes 1597448 | tf_op jit(solution)/shard_map/ppermute | solution.py:18
  26.0 20.2 %copy-start.2 = (bf16[1,64,8,32,128]{4,1,3,2,0:T(8,128)(2,1)S(1)}, bf16[1,64,8,32,128]{4,1,3,2,0:T(8,128)(2,1)}, u32[]{:S(2)}) copy-start(bf16[1,64,8,32,128]{4,1,3,2,0:T(8,128)(2,1)} %copy-done.1) | copy-start | bytes 12582916
  59.3 12.8 %copy-start.4 = (bf16[1,64,8,32,128]{4,3,2,1,0:T(8,128)(2,1)S(1)}, bf16[1,64,8,32,128]{4,3,2,1,0:T(8,128)(2,1)}, u32[]{:S(2)}) copy-start(bf16[1,64,8,32,128]{4,3,2,1,0:T(8,128)(2,1)} %param.18) | copy-start | bytes 12582916
  76.0 204.6 %all-reduce.6.cloned.1.call-start = ((), (), s32[]{:S(2)}) async-start(), calls=%async_computation.1 | async-start | bytes 1179648 | tf_op jit(solution)/shard_map/psum | solution.py:134
  76.1 3.4 %copy-start.3 = (bf16[1,64,8,32,128]{4,1,3,2,0:T(8,128)(2,1)S(1)}, bf16[1,64,8,32,128]{4,1,3,2,0:T(8,128)(2,1)}, u32[]{:S(2)}) copy-start(bf16[1,64,8,32,128]{4,1,3,2,0:T(8,128)(2,1)} %copy-done.1) | copy-start | bytes 12582916
  79.4 30.9 %copy-start.8 = (f32[1,8,32,128]{3,2,1,0:T(8,128)S(1)}, f32[1,8,32,128]{3,2,1,0:T(8,128)}, u32[]{:S(2)}) copy-start(f32[1,8,32,128]{3,2,1,0:T(8,128)} %param.14) | copy-start | bytes 393220
  79.4 30.9 %copy-start.10 = (f32[1,8,32,128]{3,2,1,0:T(8,128)S(1)}, f32[1,8,32,128]{3,2,1,0:T(8,128)}, u32[]{:S(2)}) copy-start(f32[1,8,32,128]{3,2,1,0:T(8,128)} %param.17) | copy-start | bytes 393220
  79.4 30.9 %copy-start.11 = (s32[1,8,32,128]{3,2,1,0:T(8,128)S(1)}, s32[1,8,32,128]{3,2,1,0:T(8,128)}, u32[]{:S(2)}) copy-start(s32[1,8,32,128]{3,2,1,0:T(8,128)} %param.15) | copy-start | bytes 393220
  79.4 30.9 %copy-start.14 = (f32[128]{0:T(128)S(1)}, f32[128]{0:T(128)}, u32[]{:S(2)}) copy-start(f32[128]{0:T(128)} %param.13) | copy-start | bytes 1540
  110.3 10.3 %copy-start.5 = (bf16[1,64,8,32,128]{4,3,2,1,0:T(8,128)(2,1)S(1)}, bf16[1,64,8,32,128]{4,3,2,1,0:T(8,128)(2,1)}, u32[]{:S(2)}) copy-start(bf16[1,64,8,32,128]{4,3,2,1,0:T(8,128)(2,1)} %param.18) | copy-start | bytes 12582916
  110.3 10.2 %copy-start.7 = (bf16[1,64,8,32,128]{4,3,2,1,0:T(8,128)(2,1)S(1)}, bf16[1,64,8,32,128]{4,3,2,1,0:T(8,128)(2,1)}, u32[]{:S(2)}) copy-start(bf16[1,64,8,32,128]{4,3,2,1,0:T(8,128)(2,1)} %param.11) | copy-start | bytes 12582916
  131.8 5.2 %copy-start.6 = (bf16[64,8,32,128]{3,0,2,1:T(8,128)(2,1)S(1)}, bf16[64,8,32,128]{3,0,2,1:T(8,128)(2,1)}, u32[]{:S(2)}) copy-start(bf16[64,8,32,128]{3,0,2,1:T(8,128)(2,1)} %fusion.6) | copy-start | bytes 12582916
  131.8 9.2 %slice-start = ((s8[5898240]{0:T(1024)(128)(4,1)}), s8[4194304]{0:T(1024)(128)(4,1)S(1)}, s32[]{:S(2)}) async-start(s8[5898240]{0:T(1024)(128)(4,1)} %bitcast.236), calls=%async_computation.2 | async-start | bytes 8388608
  137.0 4.0 %slice-start.1 = ((s8[5898240]{0:T(1024)(128)(4,1)}), s8[1703936]{0:T(1024)(128)(4,1)S(1)}, s32[]{:S(2)}) async-start(s8[5898240]{0:T(1024)(128)(4,1)} %bitcast.236), calls=%async_computation.3 | async-start | bytes 3407872
  144.1 3.1 slice-start.2
  153.1 129.5 %collective-permute-start.2 = (bf16[65,1,32,128]{3,2,1,0:T(8,128)(2,1)S(1)}, bf16[65,1,32,128]{3,2,1,0:T(8,128)(2,1)S(1)}, u32[]{:S(2)}, u32[]{:S(2)}) collective-permute-start(bf16[65,1,32,128]{3,2,1,0:T(8,128)(2,1)S(1)} %copy.67), channel_id=1, source_target_pairs={{0,2},{2,4},{4,6},{1,3},{3,5},{5,7},{8,10},{10,12},{12,14},{9,11},... | collective-permute-start | bytes 1597448 | tf_op jit(solution)/shard_map/ppermute | solution.py:17
  156.6 126.2 %collective-permute-start.3 = (bf16[65,1,32,128]{3,2,1,0:T(8,128)(2,1)S(1)}, bf16[65,1,32,128]{3,2,1,0:T(8,128)(2,1)S(1)}, u32[]{:S(2)}, u32[]{:S(2)}) collective-permute-start(bf16[65,1,32,128]{3,2,1,0:T(8,128)(2,1)S(1)} %copy.68), channel_id=1, source_target_pairs={{2,0},{4,2},{6,4},{3,1},{5,3},{7,5},{10,8},{12,10},{14,12},{11,9},... | collective-permute-start | bytes 1597448 | tf_op jit(solution)/shard_map/ppermute | solution.py:18
  (2 other events, 2.3 us)
Sparse Core Ops, SparseCore 0:
  76.2 34.0 all-reduce.3
  151.3 129.2 all-reduce.5
where the time goes:
time: 316 us; the launch traced here: 312 us
  matrix products  86.4 us (27%)
  waiting for transfers between devices  75 us (24%)
  blocking collectives  67.5 us (21%)
  other arithmetic  36.8 us (12%)
  local copies, waits for them, and re-layouts  20.5 us (6%)
  between operations  14.9 us (5%)
  starting transfers between devices  11.1 us (4%)
    psum x1, waiting for transfers between devices, on_device(): totals = lax.psum((grad_w_local, grad_b_local), ('gen', 'rows', 'img'))  44.6 us
    psum x1, blocking collectives, on_device(): totals = lax.psum((grad_w_local, grad_b_local), ('gen', 'rows', 'img'))  37.7 us
    psum x1, waiting for transfers between devices, on_device(): products = lax.psum(partial_sum, 'gen')  30.4 us
    all_gather x1, blocking collectives, on_device(): whole = lax.all_gather(d_rad[None], 'rows', axis=1, tiled=True)  29.8 us
    dot_general x9, matrix products, on_device(): lax.dot_general(window[1:].reshape(-1, chans), d_rows[1:].reshape(-1, cha...  27.7 us
    conv_general_dilated x2, matrix products, conv_band(): lax.conv_general_dilated(field, kernel, (1, 1), ((0, 0), (1, 1)), dimensi...  27 us
    dot_general x1, matrix products, listed_terms(): lax.dot_general(weighted, chan_table, (((0,), (0,)), ((), ())), precision...  19.7 us
    unnamed x53, local copies, waits for them, and re-layouts  13.3 us
  transfers between devices with their start and end apart: 6, of which 2 were waited for; matrix products, arithmetic and copies ran while one was open for 14% of the time, Pallas kernels for 0%

commit v1 on v0

--- a/solution.py
+++ b/solution.py
@@ -95,7 +95,7 @@
     forward = conv_band(padded, weight)
     y_center = forward[0] + bias
     partial_sum = jnp.sum(d_gens[0].astype(jnp.float32) * forward[1:], axis=0)
-    products = lax.psum(partial_sum, "gen")
+    products = jnp.sum(lax.all_gather(partial_sum, "gen"), axis=0)
     extra = listed_terms(ids, values, row_pos * band, band, width, chans)
     slope, d_yc, d_rad = relu_terms(y_center, products, radius[0], state[0], d_center[0], extra)
     d_first = jnp.concatenate(

time: 316 us -> 291 us (0.921)
  waiting for transfers between devices: 75 us -> 44.4 us
  blocking collectives: 67.5 us -> 75.9 us
  other arithmetic: 36.8 us -> 31.7 us
    psum x1 -> x0, waiting for transfers between devices: 30.4 us -> none  [on_device(): products = lax.psum(partial_sum, 'gen')]
    all_gather x0 -> x1, blocking collectives: none -> 7.2 us  [on_device(): products = jnp.sum(lax.all_gather(partial_sum, 'gen'), axis=0)]
    unnamed x53 -> x59, local copies, waits for them, and re-layouts: 13.3 us -> 14.6 us
  transfers between devices with their start and end apart: 6 -> 5, of which waited for: 2 -> 1; matrix products, arithmetic and copies ran while one was open for 14% -> 14% of each run, Pallas kernels for 0% -> 0%
where the time goes in v1:
time: 291 us; the launch traced here: 287 us
  matrix products  87.3 us (30%)
  blocking collectives  75.9 us (26%)
  waiting for transfers between devices  44.4 us (15%)
  other arithmetic  31.7 us (11%)
  local copies, waits for them, and re-layouts  20.1 us (7%)
  between operations  15 us (5%)
  starting transfers between devices  12.2 us (4%)
    psum x1, waiting for transfers between devices, on_device(): totals = lax.psum((grad_w_local, grad_b_local), ('gen', 'rows', 'img'))  44.4 us
    psum x1, blocking collectives, on_device(): totals = lax.psum((grad_w_local, grad_b_local), ('gen', 'rows', 'img'))  37.8 us
    all_gather x1, blocking collectives, on_device(): whole = lax.all_gather(d_rad[None], 'rows', axis=1, tiled=True)  30.9 us
    dot_general x9, matrix products, on_device(): lax.dot_general(window[1:].reshape(-1, chans), d_rows[1:].reshape(-1, cha...  28.5 us
    conv_general_dilated x2, matrix products, conv_band(): lax.conv_general_dilated(field, kernel, (1, 1), ((0, 0), (1, 1)), dimensi...  27.2 us
    dot_general x1, matrix products, listed_terms(): lax.dot_general(weighted, chan_table, (((0,), (0,)), ((), ())), precision...  19.7 us
    unnamed x59, local copies, waits for them, and re-layouts  14.6 us
    concatenate x2, other arithmetic, with_halo(): array = jnp.concatenate([before, array, after], axis=dim)  12.7 us
  transfers between devices with their start and end apart: 5, of which 1 were waited for; matrix products, arithmetic and copies ran while one was open for 14% of the time, Pallas kernels for 0%

profile of v1, /device:TPU:0, one launch (start us, length us, event | category | flops | bytes accessed | tf_op | source)
XLA Modules:
  0.0 286.7 jit_solution(16348776774069506849)
XLA Ops:
  7.2 4.9 %copy.127 = bf16[1,64,8,32,128]{4,1,3,2,0:T(8,128)(2,1)S(1)} copy(bf16[1,64,8,32,128]{4,3,2,1,0:T(8,128)(2,1)} %param.11) | data formatting | bytes 8388608 | tf_op args[1]
  12.3 1.9 copy-done.1
  14.8 5.0 %collective-permute-start = (bf16[65,1,32,128]{3,2,1,0:T(8,128)(2,1)S(1)}, bf16[65,1,32,128]{3,2,1,0:T(8,128)(2,1)S(1)}, u32[]{:S(2)}, u32[]{:S(2)}) collective-permute-start(bf16[65,1,32,128]{3,2,1,0:T(8,128)(2,1)S(1)} %copy.82), channel_id=1, source_target_pairs={{0,2},{2,4},{4,6},{1,3},{3,5},{5,7},{8,10},{10,12},{12,14},{9,11},... | collective-permute-start | bytes 1597448 | tf_op jit(solution)/shard_map/ppermute | solution.py:17
  21.3 5.0 %iota_compare_fusion.14 = pred[16384,128]{1,0:T(32,128)(4,1)} fusion(s32[16384]{0:T(1024)S(1)} %get-tuple-element.44), kind=kLoop, calls=%fused_computation.13.clone.clone.2 | loop fusion | flops 2097152 | bytes 2162688 | tf_op jit(solution)/shard_map/dot_general | solution.py:51
  26.3 19.7 %fusion = f32[256,128]{1,0:T(8,128)S(1)} fusion(f32[16384]{0:T(1024)S(1)} %bitcast.312, s32[16384]{0:T(1024)S(1)} %get-tuple-element.45, pred[16384,128]{1,0:T(32,128)(4,1)} %iota_compare_fusion.14), kind=kOutput, calls=%fused_computation.1 | convolution fusion | flops 6450839552 | bytes 2359296 | tf_op jit(solution)/shard_map/dot_general | solution.py:51
  47.6 4.9 %pad_maximum_fusion = bf16[65,10,32,128]{3,0,2,1:T(8,128)(2,1)} fusion(bf16[65,1,32,128]{3,0,2,1:T(8,128)(2,1)S(1)} %copy.85, bf16[64,8,32,128]{3,0,2,1:T(8,128)(2,1)S(1)} %bitcast.280, bf16[1,8,32,128]{3,0,2,1:T(2,128)(2,1)S(1)} %copy.81, bf16[65,1,32,128]{3,0,2,1:T(8,128)(2,1)S(1)} %copy.84), kind=kLoop, calls=%fused_computation.17 | loop fusion | flops 21299200 | bytes 10649600 | tf_op jit(solution)/shard_map/concatenate | solution.py:19
  52.7 12.9 %fusion.192 = f32[65,8,32,128]{3,0,2,1:T(8,128)S(1)} fusion(bf16[3,3,128,128]{3,2,1,0:T(8,128)(2,1)S(1)} %copy-done, bf16[65,1,32,128]{3,0,2,1:T(8,128)(2,1)S(1)} %copy.85, bf16[64,8,32,128]{3,0,2,1:T(8,128)(2,1)S(1)} %bitcast.282, bf16[1,8,32,128]{3,0,2,1:T(2,128)(2,1)S(1)} %copy.81, bf16[65,1,32,128]{3,0,2,1:T(8,128)(2,1)S(1)} %copy.84), kind=kOutput, calls=%fused_computation.192 | convolution fusion | flops 4826398720 | bytes 14139392 | tf_op jit(solution)/shard_map/conv_general_dilated | solution.py:24
  65.8 3.2 %fusion.5 = f32[8,32,128]{2,1,0:T(8,128)S(1)} fusion(f32[65,8,32,128]{3,0,2,1:T(8,128)S(1)} %fusion.192, bf16[1,64,8,32,128]{4,3,2,1,0:T(8,128)(2,1)S(1)} %copy-done.4), kind=kLoop, calls=%fused_computation.9 | loop fusion | flops 6258688 | bytes 12713984 | tf_op jit(solution)/shard_map/reduce_sum | solution.py:97
  69.0 7.2 %all-gather = f32[32,32,128]{2,1,0:T(8,128)S(1)} all-gather(f32[8,32,128]{2,1,0:T(8,128)S(1)} %fusion.5), channel_id=2, replica_groups=mesh['gen'=4,'rows'=4,'img'=2] {'gen'}, dimensions={0}, use_global_device_ids=true | all-gather | bytes 655360 | tf_op jit(solution)/shard_map/all_gather | solution.py:98
  76.5 12.6 %fusion.73 = f32[128,128]{1,0:T(8,128)S(1)} fusion(f32[8,32,128]{2,1,0:T(8,128)S(1)} %get-tuple-element.42, bf16[1,64,8,32,128]{4,3,2,1,0:T(8,128)(2,1)} %param.18, bf16[1,64,8,32,128]{4,3,2,1,0:T(8,128)(2,1)} %param.11), kind=kOutput, calls=%fused_computation.74 | convolution fusion | flops 543162368 | bytes 8585216 | tf_op jit(solution)/shard_map/dot_general | solution.py:122
  89.1 5.3 %fusion.6 = bf16[64,8,32,128]{3,0,2,1:T(8,128)(2,1)} fusion(f32[8,32,128]{2,1,0:T(8,128)S(1)} %get-tuple-element.42, bf16[1,64,8,32,128]{4,3,2,1,0:T(8,128)(2,1)S(1)} %copy-done.5), kind=kLoop, calls=%fused_computation.10 | loop fusion | flops 6291456 | bytes 8519680 | tf_op jit(solution)/shard_map/convert_element_type | solution.py:104
  94.5 7.8 %pad_maximum_fusion.1 = (bf16[65,9,32,128]{3,0,2,1:T(8,128)(2,1)}, bf16[65,9,32,128]{3,0,2,1:T(8,128)(2,1)}) fusion(bf16[65,1,32,128]{3,0,2,1:T(8,128)(2,1)S(1)} %copy.85, bf16[64,8,32,128]{3,0,2,1:T(8,128)(2,1)S(1)} %bitcast.283, bf16[1,8,32,128]{3,0,2,1:T(2,128)(2,1)S(1)} %copy.81, bf16[65,1,32,128]{3,0,2,1:T(8,128)(2,1)S(1)} %copy.84), kind=kLoop, calls=%fused_computation.27 | loop fusion | flops 28753920 | bytes 14909440 | tf_op jit(solution)/shard_map/concatenate | solution.py:19
  105.0 5.2 %fusion.145 = f32[9,128,128]{2,1,0:T(8,128)S(1)} fusion(f32[128,128]{1,0:T(8,128)S(1)} %convolution_multiply_fusion.8, bf16[64,8,32,128]{3,0,2,1:T(8,128)(2,1)} %fusion.6, bf16[65,10,32,128]{3,0,2,1:T(8,128)(2,1)} %pad_maximum_fusion), kind=kOutput, calls=%fused_computation.98 | convolution fusion | flops 536887296 | bytes 9650176 | tf_op jit(solution)/shard_map/dot_general | solution.py:122
  120.6 1.8 fusion.100
  123.5 1.6 pad_maximum_fusion.3
  125.2 4.6 %collective-permute-start.2 = (bf16[65,1,32,128]{3,2,1,0:T(8,128)(2,1)S(1)}, bf16[65,1,32,128]{3,2,1,0:T(8,128)(2,1)S(1)}, u32[]{:S(2)}, u32[]{:S(2)}) collective-permute-start(bf16[65,1,32,128]{3,2,1,0:T(8,128)(2,1)S(1)} %copy.89), channel_id=1, source_target_pairs={{0,2},{2,4},{4,6},{1,3},{3,5},{5,7},{8,10},{10,12},{12,14},{9,11},... | collective-permute-start | bytes 1597448 | tf_op jit(solution)/shard_map/ppermute | solution.py:17
  131.2 30.9 %all_gather.11 = f32[1,32,32,128]{3,2,0,1:T(8,128)S(1)} all-gather(f32[1,8,32,128]{3,2,0,1:T(8,128)S(1)} %get-tuple-element.25), channel_id=1, replica_groups=mesh['gen'=4,'rows'=4,'img'=2] {'rows'}, dimensions={1}, use_global_device_ids=true | all-gather | bytes 655360 | tf_op jit(solution)/shard_map/all_gather | solution.py:139
  162.1 10.2 %fusion.46 = f32[4096]{0:T(1024)} fusion(f32[1024,128]{1,0:T(8,128)S(1)} %bitcast.300, s32[4096]{0:T(1024)S(1)} %get-tuple-element.47, s32[4096]{0:T(1024)S(1)} %get-tuple-element.46), kind=kOutput, calls=%fused_computation.54 | convolution fusion | flops 6448214016 | bytes 573440 | tf_op jit(solution)/shard_map/dot_general | solution.py:63
  172.2 37.8 %psum.15 = f32[128]{0:T(128)S(1)} all-reduce(f32[128]{0:T(128)S(1)} %broadcast_multiply_fusion.2), channel_id=1, replica_groups=mesh['gen'=4,'rows'=4,'img'=2] {'gen','rows','img'}, use_global_device_ids=true, to_apply=%region_4.5 | all-reduce | flops 128 | bytes 1024 | tf_op jit(solution)/shard_map/psum | solution.py:134
  210.6 44.4 %all-reduce.3.cloned.1.call-done = f32[3,3,128,128]{3,2,1,0:T(8,128)} async-done(((f32[3,3,128,128]{3,2,1,0:T(8,128)}), f32[3,3,128,128]{3,2,1,0:T(8,128)}) %all-reduce.3.cloned.1.call-update) | async-done | bytes 589840 | tf_op jit(solution)/shard_map/psum | solution.py:134
  255.0 1.9 broadcast_multiply_fusion
  257.4 14.3 %fusion.43 = bf16[65,8,32,128]{3,0,2,1:T(8,128)(2,1)S(1)} fusion(bf16[3,3,128,128]{3,2,1,0:T(8,128)(2,1)S(1)} %copy-done, bf16[65,1,32,128]{3,0,2,1:T(8,128)(2,1)S(1)} %copy.92, bf16[64,8,32,128]{3,0,2,1:T(8,128)(2,1)} %fusion.6, bf16[1,8,32,128]{3,0,2,1:T(2,128)(2,1)S(1)} %copy.88, bf16[65,1,32,128]{3,0,2,1:T(8,128)(2,1)S(1)} %copy.91), kind=kOutput, calls=%fused_computation.52 | convolution fusion | flops 4828528640 | bytes 9879552 | tf_op jit(solution)/shard_map/conv_general_dilated | solution.py:24
  271.7 2.4 slice_bitcast_fusion
  274.2 4.7 %copy.98 = bf16[1,64,8,32,128]{4,3,2,1,0:T(8,128)(2,1)} copy(bf16[1,64,8,32,128]{4,1,3,2,0:T(8,128)(2,1)S(1)} %slice_bitcast_fusion) | data formatting | bytes 8388608
  (108 shorter events, 21.5 us)
Async XLA Ops:
  7.2 45.5 %copy-start = (bf16[3,3,128,128]{3,2,1,0:T(8,128)(2,1)S(1)}, bf16[3,3,128,128]{3,2,1,0:T(8,128)(2,1)}, u32[]{:S(2)}) copy-start(bf16[3,3,128,128]{3,2,1,0:T(8,128)(2,1)} %param.12) | copy-start | bytes 884740
  7.2 5.0 %copy-start.11 = (bf16[1,8,32,128]{3,2,1,0:T(8,128)(2,1)S(1)}, bf16[1,8,32,128]{3,2,1,0:T(8,128)(2,1)}, u32[]{:S(2)}) copy-start(bf16[1,8,32,128]{3,2,1,0:T(8,128)(2,1)} %param.10) | copy-start | bytes 196612
  7.2 247.8 %all-reduce.3.cloned.1.call-start = ((), (), s32[]{:S(2)}) async-start(), calls=%async_computation | async-start | bytes 1179648 | tf_op jit(solution)/shard_map/psum | solution.py:134
  12.2 9.0 %copy-start.12 = (s32[1,16384]{1,0:T(1,128)S(1)}, s32[1,16384]{1,0:T(1,128)}, u32[]{:S(2)}) copy-start(s32[1,16384]{1,0:T(1,128)} %param.16) | copy-start | bytes 196612
  12.2 14.1 %copy-start.14 = (f32[1,16384]{1,0:T(1,128)S(1)}, f32[1,16384]{1,0:T(1,128)}, u32[]{:S(2)}) copy-start(f32[1,16384]{1,0:T(1,128)} %param.19) | copy-start | bytes 196612
  14.8 31.2 %collective-permute-start = (bf16[65,1,32,128]{3,2,1,0:T(8,128)(2,1)S(1)}, bf16[65,1,32,128]{3,2,1,0:T(8,128)(2,1)S(1)}, u32[]{:S(2)}, u32[]{:S(2)}) collective-permute-start(bf16[65,1,32,128]{3,2,1,0:T(8,128)(2,1)S(1)} %copy.82), channel_id=1, source_target_pairs={{0,2},{2,4},{4,6},{1,3},{3,5},{5,7},{8,10},{10,12},{12,14},{9,11},... | collective-permute-start | bytes 1597448 | tf_op jit(solution)/shard_map/ppermute | solution.py:17
  19.9 26.4 %collective-permute-start.1 = (bf16[65,1,32,128]{3,2,1,0:T(8,128)(2,1)S(1)}, bf16[65,1,32,128]{3,2,1,0:T(8,128)(2,1)}, u32[]{:S(2)}, u32[]{:S(2)}) collective-permute-start(bf16[65,1,32,128]{3,2,1,0:T(8,128)(2,1)S(1)} %copy.83), channel_id=1, source_target_pairs={{2,0},{4,2},{6,4},{3,1},{5,3},{7,5},{10,8},{12,10},{14,12},{11,9},... | collective-permute-start | bytes 1597448 | tf_op jit(solution)/shard_map/ppermute | solution.py:18
  26.3 21.2 %copy-start.2 = (bf16[1,64,8,32,128]{4,1,3,2,0:T(8,128)(2,1)S(1)}, bf16[1,64,8,32,128]{4,1,3,2,0:T(8,128)(2,1)}, u32[]{:S(2)}) copy-start(bf16[1,64,8,32,128]{4,1,3,2,0:T(8,128)(2,1)} %copy-done.1) | copy-start | bytes 12582916
  52.7 13.0 %copy-start.4 = (bf16[1,64,8,32,128]{4,3,2,1,0:T(8,128)(2,1)S(1)}, bf16[1,64,8,32,128]{4,3,2,1,0:T(8,128)(2,1)}, u32[]{:S(2)}) copy-start(bf16[1,64,8,32,128]{4,3,2,1,0:T(8,128)(2,1)} %param.18) | copy-start | bytes 12582916
  65.7 10.5 %copy-start.7 = (f32[1,8,32,128]{3,2,1,0:T(8,128)S(1)}, f32[1,8,32,128]{3,2,1,0:T(8,128)}, u32[]{:S(2)}) copy-start(f32[1,8,32,128]{3,2,1,0:T(8,128)} %param.14) | copy-start | bytes 393220
  65.7 10.5 %copy-start.8 = (f32[1,8,32,128]{3,2,1,0:T(8,128)S(1)}, f32[1,8,32,128]{3,2,1,0:T(8,128)}, u32[]{:S(2)}) copy-start(f32[1,8,32,128]{3,2,1,0:T(8,128)} %param.17) | copy-start | bytes 393220
  65.7 10.5 %copy-start.9 = (s32[1,8,32,128]{3,2,1,0:T(8,128)S(1)}, s32[1,8,32,128]{3,2,1,0:T(8,128)}, u32[]{:S(2)}) copy-start(s32[1,8,32,128]{3,2,1,0:T(8,128)} %param.15) | copy-start | bytes 393220
  65.8 10.5 %copy-start.13 = (f32[128]{0:T(128)S(1)}, f32[128]{0:T(128)}, u32[]{:S(2)}) copy-start(f32[128]{0:T(128)} %param.13) | copy-start | bytes 1540
  76.5 12.6 %copy-start.5 = (bf16[1,64,8,32,128]{4,3,2,1,0:T(8,128)(2,1)S(1)}, bf16[1,64,8,32,128]{4,3,2,1,0:T(8,128)(2,1)}, u32[]{:S(2)}) copy-start(bf16[1,64,8,32,128]{4,3,2,1,0:T(8,128)(2,1)} %param.18) | copy-start | bytes 12582916
  89.1 5.4 %copy-start.3 = (bf16[1,64,8,32,128]{4,1,3,2,0:T(8,128)(2,1)S(1)}, bf16[1,64,8,32,128]{4,1,3,2,0:T(8,128)(2,1)}, u32[]{:S(2)}) copy-start(bf16[1,64,8,32,128]{4,1,3,2,0:T(8,128)(2,1)} %copy-done.1) | copy-start | bytes 12582916
  89.1 13.2 %slice-start = ((s8[5898240]{0:T(1024)(128)(4,1)}), s8[4194304]{0:T(1024)(128)(4,1)S(1)}, s32[]{:S(2)}) async-start(s8[5898240]{0:T(1024)(128)(4,1)} %bitcast.284), calls=%async_computation.1 | async-start | bytes 8388608
  94.5 7.8 %slice-start.1 = ((s8[5898240]{0:T(1024)(128)(4,1)}), s8[1703936]{0:T(1024)(128)(4,1)S(1)}, s32[]{:S(2)}) async-start(s8[5898240]{0:T(1024)(128)(4,1)} %bitcast.284), calls=%async_computation.2 | async-start | bytes 3407872
  104.8 5.4 %slice-start.6 = ((s8[5308416]{0:T(1024)(128)(4,1)}), s8[4194304]{0:T(1024)(128)(4,1)S(1)}, s32[]{:S(2)}) async-start(s8[5308416]{0:T(1024)(128)(4,1)} %bitcast.290), calls=%async_computation.7 | async-start | bytes 8388608
  105.0 5.9 %copy-start.6 = (bf16[64,8,32,128]{3,0,2,1:T(8,128)(2,1)S(1)}, bf16[64,8,32,128]{3,0,2,1:T(8,128)(2,1)}, u32[]{:S(2)}) copy-start(bf16[64,8,32,128]{3,0,2,1:T(8,128)(2,1)} %fusion.6) | copy-start | bytes 12582916
  105.0 6.1 %slice-start.7 = ((s8[5308416]{0:T(1024)(128)(4,1)}), s8[1114112]{0:T(1024)(128)(4,1)S(1)}, s32[]{:S(2)}) async-start(s8[5308416]{0:T(1024)(128)(4,1)} %bitcast.290), calls=%async_computation.8 | async-start | bytes 2228224
  105.0 7.6 %slice-start.2 = ((s8[5898240]{0:T(1024)(128)(4,1)}), s8[4194304]{0:T(1024)(128)(4,1)S(1)}, s32[]{:S(2)}) async-start(s8[5898240]{0:T(1024)(128)(4,1)} %bitcast.286), calls=%async_computation.3 | async-start | bytes 8388608
  116.0 3.1 %slice-start.4 = ((s8[5308416]{0:T(1024)(128)(4,1)}), s8[4194304]{0:T(1024)(128)(4,1)S(1)}, s32[]{:S(2)}) async-start(s8[5308416]{0:T(1024)(128)(4,1)} %bitcast.288), calls=%async_computation.5 | async-start | bytes 8388608
  125.2 131.7 %collective-permute-start.2 = (bf16[65,1,32,128]{3,2,1,0:T(8,128)(2,1)S(1)}, bf16[65,1,32,128]{3,2,1,0:T(8,128)(2,1)S(1)}, u32[]{:S(2)}, u32[]{:S(2)}) collective-permute-start(bf16[65,1,32,128]{3,2,1,0:T(8,128)(2,1)S(1)} %copy.89), channel_id=1, source_target_pairs={{0,2},{2,4},{4,6},{1,3},{3,5},{5,7},{8,10},{10,12},{12,14},{9,11},... | collective-permute-start | bytes 1597448 | tf_op jit(solution)/shard_map/ppermute | solution.py:17
  129.9 127.3 %collective-permute-start.3 = (bf16[65,1,32,128]{3,2,1,0:T(8,128)(2,1)S(1)}, bf16[65,1,32,128]{3,2,1,0:T(8,128)(2,1)S(1)}, u32[]{:S(2)}, u32[]{:S(2)}) collective-permute-start(bf16[65,1,32,128]{3,2,1,0:T(8,128)(2,1)S(1)} %copy.90), channel_id=1, source_target_pairs={{2,0},{4,2},{6,4},{3,1},{5,3},{7,5},{10,8},{12,10},{14,12},{11,9},... | collective-permute-start | bytes 1597448 | tf_op jit(solution)/shard_map/ppermute | solution.py:18
  (4 other events, 6.2 us)
Sparse Core Ops, SparseCore 0:
  123.3 131.5 all-reduce.2
